TPU v7x, 32 devices: a whole 2x2x4 slice. The times are simulated.
32 devices in a mesh: dp: 8 (over z, x), tensor: 4 (over y, core).
Axes of the slice: x: 2, y: 2, z: 4, core: 2. Of those that a mesh axis runs over, the one named last changes fastest.
Arguments:
- tokens: bfloat16 [12288, 768], P('dp'), may hold values from -6 to 6
- grad_out: bfloat16 [12288, 768], P('dp'), may hold values from -8 to 8
- token_weight: float32 [12288], P('dp'), may hold values from 0.5 to 2
- lengths: int32 [24], P('dp'), may hold values from 1 to 512, 6144 in all
- step: int32 [1], replicated, may hold values from 2 to 20
- qkv_weight: bfloat16 [3, 768, 768], P(None, 'dp', 'tensor'), may hold values from -0.21875 to 0.21875
- out_weight: bfloat16 [768, 768], P('tensor', 'dp'), may hold values from -1.75 to 1.75
- up_weight: bfloat16 [768, 3072], P('dp', 'tensor'), may hold values from -0.21875 to 0.21875
- down_weight: bfloat16 [3072, 768], P('tensor', 'dp'), may hold values from -0.109375 to 0.109375
- norm_params: bfloat16 [4, 768], P(None, 'dp'), may hold values from 0.5 to 1.5
- first_qkv: float32 [3, 768, 768], P(None, 'dp', 'tensor'), may hold values from -32 to 32
- first_out: float32 [768, 768], P('tensor', 'dp'), may hold values from -4 to 4
- first_up: float32 [768, 3072], P('dp', 'tensor'), may hold values from -20 to 20
- first_down: float32 [3072, 768], P('tensor', 'dp'), may hold values from -40 to 40
- first_norm: float32 [4, 768], P(None, 'dp'), may hold values from -56 to 56
- second_qkv: float32 [3, 768, 768], P(None, 'dp', 'tensor'), may hold values from 143.21678 to 572.8671
- second_out: float32 [768, 768], P('tensor', 'dp'), may hold values from 2.2413425 to 8.951049
- second_up: float32 [768, 3072], P('dp', 'tensor'), may hold values from 57.01632 to 227.9424
- second_down: float32 [3072, 768], P('tensor', 'dp'), may hold values from 191.6928 to 768
- second_norm: float32 [4, 768], P(None, 'dp'), may hold values from 391.3728 to 1566.72
Outputs:
- output: bfloat16 [12288, 768], P('dp')
- grad_input: float32 [12288, 768], P('dp')
- new_qkv: float32 [3, 768, 768], P(None, 'dp', 'tensor')
- moment_qkv: float32 [3, 768, 768], P(None, 'dp', 'tensor')
- square_qkv: float32 [3, 768, 768], P(None, 'dp', 'tensor')
- copy_qkv: bfloat16 [3, 768, 768], P(None, 'dp', 'tensor')
- new_out: float32 [768, 768], P('tensor', 'dp')
- moment_out: float32 [768, 768], P('tensor', 'dp')
- square_out: float32 [768, 768], P('tensor', 'dp')
- copy_out: bfloat16 [768, 768], P('tensor', 'dp')
- new_up: float32 [768, 3072], P('dp', 'tensor')
- moment_up: float32 [768, 3072], P('dp', 'tensor')
- square_up: float32 [768, 3072], P('dp', 'tensor')
- copy_up: bfloat16 [768, 3072], P('dp', 'tensor')
- new_down: float32 [3072, 768], P('tensor', 'dp')
- moment_down: float32 [3072, 768], P('tensor', 'dp')
- square_down: float32 [3072, 768], P('tensor', 'dp')
- copy_down: bfloat16 [3072, 768], P('tensor', 'dp')
- new_norm: float32 [4, 768], P(None, 'dp')
- moment_norm: float32 [4, 768], P(None, 'dp')
- square_norm: float32 [4, 768], P(None, 'dp')
- copy_norm: bfloat16 [4, 768], P(None, 'dp')
Inputs may be any that keep to these rules, and one draw needn't show every extreme that they name: `lengths`: used tokens of each sequence; one sequence uses all 512 slots.
All inputs are finite; a program needn't handle non-finite values. No bound on the sum of `lengths` on one device may be relied on, other than what follows from the above.
Results may differ from a plain program's by a relative error of at most 0.014.
Values may be sent and summed in bfloat16 or wider, within the bound.
No kernel may reach another device: no remote copies, remote signals or barrier semaphores. Data moves between devices by JAX's collectives and lax.ppermute only.
A program may use at most 128 MiB of HBM per device.

v0:
```python
import jax
import jax.numpy as jnp
from jax import lax
from jax.sharding import PartitionSpec as P

HD = 64
NORM_EPS = 1e-05
BETA_ONE = 0.9
BETA_TWO = 0.95
ADAM_EPS = 1e-08
DECAY_RATE = 0.01
PEAK_RATE = 0.15
WARM_STEPS = 2.0
LAST_STEP = 40.0
MASK_VALUE = -1000000000.0


def exact_gelu(values):
    return jax.nn.gelu(values, approximate=False)


def norm_forward(summed, gain, shift):
    center = summed - jnp.mean(summed, axis=-1, keepdims=True)
    inverse = lax.rsqrt(jnp.mean(center * center, axis=-1, keepdims=True) + NORM_EPS)
    normed = center * inverse
    return (normed * gain + shift, normed, inverse)


def norm_backward(upstream, normed, inverse, gain):
    scaled = upstream * gain
    inner = (
        scaled
        - jnp.mean(scaled, axis=-1, keepdims=True)
        - normed * jnp.mean(scaled * normed, axis=-1, keepdims=True)
    )
    return (inner * inverse, jnp.sum(upstream * normed, axis=0), jnp.sum(upstream, axis=0))


def adamw_update(gradient, weight_low, first, second, rate, fix_one, fix_two, decay):
    weight = weight_low.astype(jnp.float32)
    first_new = BETA_ONE * first + (1.0 - BETA_ONE) * gradient
    second_new = BETA_TWO * second + (1.0 - BETA_TWO) * gradient * gradient
    direction = first_new / fix_one / (jnp.sqrt(second_new / fix_two) + ADAM_EPS)
    weight_new = weight - rate * (direction + decay * weight)
    return (weight_new, first_new, second_new, weight_new.astype(jnp.bfloat16))


def on_device(
    tokens,
    grad_out,
    token_weight,
    lengths,
    step,
    qkv_weight,
    out_weight,
    up_weight,
    down_weight,
    norm_params,
    first_qkv,
    first_out,
    first_up,
    first_down,
    first_norm,
    second_qkv,
    second_out,
    second_up,
    second_down,
    second_norm,
):
    qkv_full, out_full, up_full, down_full, norm_full = (
        lax.all_gather(qkv_weight, "dp", axis=1, tiled=True),
        lax.all_gather(out_weight, "dp", axis=1, tiled=True),
        lax.all_gather(up_weight, "dp", axis=0, tiled=True),
        lax.all_gather(down_weight, "dp", axis=1, tiled=True),
        lax.all_gather(norm_params, "dp", axis=1, tiled=True),
    )
    norm_float = norm_full.astype(jnp.float32)
    seq_count = lengths.shape[0]
    tok_count = tokens.shape[0]
    seq_len = tok_count // seq_count
    local_width = qkv_full.shape[2]
    local_heads = local_width // HD
    score_scale = HD ** (-0.5)
    tok_float = tokens.astype(jnp.float32)
    projected = jnp.einsum(
        "td,cde->cte", tokens, qkv_full, preferred_element_type=jnp.float32
    ).astype(jnp.bfloat16)
    split_heads = projected.reshape(3, seq_count, seq_len, local_heads, HD)
    queries, key_rows, value_rows = (split_heads[0], split_heads[1], split_heads[2])
    key_valid = jnp.arange(seq_len, dtype=jnp.int32)[None, :] < lengths[:, None]
    key_mask = key_valid[:, None, None, :]

    def attention_scores():
        raw_scores = jnp.einsum(
            "sqhe,skhe->shqk", queries, key_rows, preferred_element_type=jnp.float32
        )
        return jnp.where(key_mask, raw_scores * score_scale, MASK_VALUE)

    first_scores = attention_scores()
    log_total = jax.nn.logsumexp(first_scores, axis=-1, keepdims=True)
    probs_low = jnp.exp(first_scores - log_total).astype(jnp.bfloat16)
    context = jnp.einsum(
        "shqk,skhe->sqhe", probs_low, value_rows, preferred_element_type=jnp.float32
    )
    context_low = context.reshape(tok_count, local_width).astype(jnp.bfloat16)
    attn_part = jnp.dot(context_low, out_full, preferred_element_type=jnp.float32)
    attn_total = lax.psum(attn_part, "tensor")
    hidden_one, normed_one, inverse_one = norm_forward(
        tok_float + attn_total, norm_float[0], norm_float[1]
    )
    hidden_mine = hidden_one.astype(jnp.bfloat16)
    up_value = jnp.dot(hidden_mine, up_full, preferred_element_type=jnp.float32)
    gelu_value, gelu_pull = jax.vjp(exact_gelu, up_value)
    inner_low = gelu_value.astype(jnp.bfloat16)
    ffn_part = jnp.dot(inner_low, down_full, preferred_element_type=jnp.float32)
    ffn_total = lax.psum(ffn_part, "tensor")
    result, normed_two, inverse_two = norm_forward(
        hidden_one + ffn_total, norm_float[2], norm_float[3]
    )
    tok_valid = key_valid.reshape(tok_count).astype(jnp.float32)
    upstream = grad_out.astype(jnp.float32) * token_weight[:, None] * tok_valid[:, None]
    grad_two, gain_two, shift_two = norm_backward(upstream, normed_two, inverse_two, norm_float[2])
    ffn_mine = grad_two.astype(jnp.bfloat16)
    grad_down = jnp.einsum("tf,td->fd", inner_low, ffn_mine, preferred_element_type=jnp.float32)
    grad_inner = jnp.dot(ffn_mine, down_full.T, preferred_element_type=jnp.float32)
    up_low = gelu_pull(grad_inner)[0].astype(jnp.bfloat16)
    grad_up = jnp.einsum("td,tf->df", hidden_mine, up_low, preferred_element_type=jnp.float32)
    hidden_part = jnp.dot(up_low, up_full.T, preferred_element_type=jnp.float32)
    hidden_grad = grad_two + lax.psum(hidden_part, "tensor")
    grad_one, gain_one, shift_one = norm_backward(
        hidden_grad, normed_one, inverse_one, norm_float[0]
    )
    attn_mine = grad_one.astype(jnp.bfloat16)
    grad_outw = jnp.einsum("te,td->ed", context_low, attn_mine, preferred_element_type=jnp.float32)
    context_grad = jnp.dot(attn_mine, out_full.T, preferred_element_type=jnp.float32).astype(
        jnp.bfloat16
    )
    context_grad = context_grad.reshape(seq_count, seq_len, local_heads, HD)
    probs = jnp.exp(attention_scores() - log_total)
    probs_again = probs.astype(jnp.bfloat16)
    probs_grad = jnp.einsum(
        "sqhe,skhe->shqk", context_grad, value_rows, preferred_element_type=jnp.float32
    )
    value_grad = jnp.einsum(
        "shqk,sqhe->skhe", probs_again, context_grad, preferred_element_type=jnp.float32
    )
    score_grad = (
        probs * (probs_grad - jnp.sum(probs_grad * probs, axis=-1, keepdims=True)) * score_scale
    ).astype(jnp.bfloat16)
    query_grad = jnp.einsum(
        "shqk,skhe->sqhe", score_grad, key_rows, preferred_element_type=jnp.float32
    )
    key_grad = jnp.einsum(
        "shqk,sqhe->skhe", score_grad, queries, preferred_element_type=jnp.float32
    )
    proj_grad = (
        jnp.stack([query_grad, key_grad, value_grad])
        .astype(jnp.bfloat16)
        .reshape(3, tok_count, local_width)
    )
    grad_qkv = jnp.einsum("td,cte->cde", tokens, proj_grad, preferred_element_type=jnp.float32)
    input_part = jnp.einsum("cte,cde->td", proj_grad, qkv_full, preferred_element_type=jnp.float32)
    norm_partial = jnp.stack([gain_one, shift_one, gain_two, shift_two])
    result_low = result.astype(jnp.bfloat16)
    input_grad = grad_one + lax.psum(input_part, "tensor")
    shard_qkv, shard_out, shard_up, shard_down, shard_norm = (
        lax.psum_scatter(grad_qkv, "dp", scatter_dimension=1, tiled=True),
        lax.psum_scatter(grad_outw, "dp", scatter_dimension=1, tiled=True),
        lax.psum_scatter(grad_up, "dp", scatter_dimension=0, tiled=True),
        lax.psum_scatter(grad_down, "dp", scatter_dimension=1, tiled=True),
        lax.psum_scatter(norm_partial, "dp", scatter_dimension=1, tiled=True),
    )
    step_float = step[0].astype(jnp.float32)
    rate = PEAK_RATE * jnp.minimum(
        step_float / WARM_STEPS, (LAST_STEP - step_float) / (LAST_STEP - WARM_STEPS)
    )
    fix_one = 1.0 - BETA_ONE**step_float
    fix_two = 1.0 - BETA_TWO**step_float
    upd_qkv = adamw_update(
        shard_qkv, qkv_weight, first_qkv, second_qkv, rate, fix_one, fix_two, DECAY_RATE
    )
    upd_out = adamw_update(
        shard_out, out_weight, first_out, second_out, rate, fix_one, fix_two, DECAY_RATE
    )
    upd_up = adamw_update(
        shard_up, up_weight, first_up, second_up, rate, fix_one, fix_two, DECAY_RATE
    )
    upd_down = adamw_update(
        shard_down, down_weight, first_down, second_down, rate, fix_one, fix_two, DECAY_RATE
    )
    upd_norm = adamw_update(
        shard_norm, norm_params, first_norm, second_norm, rate, fix_one, fix_two, 0.0
    )
    return (
        result_low,
        input_grad,
        upd_qkv[0],
        upd_qkv[1],
        upd_qkv[2],
        upd_qkv[3],
        upd_out[0],
        upd_out[1],
        upd_out[2],
        upd_out[3],
        upd_up[0],
        upd_up[1],
        upd_up[2],
        upd_up[3],
        upd_down[0],
        upd_down[1],
        upd_down[2],
        upd_down[3],
        upd_norm[0],
        upd_norm[1],
        upd_norm[2],
        upd_norm[3],
    )


def solution(mesh):
    return jax.shard_map(
        on_device,
        mesh=mesh,
        in_specs=(
            P("dp", None),
            P("dp", None),
            P("dp"),
            P("dp"),
            P(),
            P(None, "dp", "tensor"),
            P("tensor", "dp"),
            P("dp", "tensor"),
            P("tensor", "dp"),
            P(None, "dp"),
            P(None, "dp", "tensor"),
            P("tensor", "dp"),
            P("dp", "tensor"),
            P("tensor", "dp"),
            P(None, "dp"),
            P(None, "dp", "tensor"),
            P("tensor", "dp"),
            P("dp", "tensor"),
            P("tensor", "dp"),
            P(None, "dp"),
        ),
        out_specs=(
            P("dp", None),
            P("dp", None),
            P(None, "dp", "tensor"),
            P(None, "dp", "tensor"),
            P(None, "dp", "tensor"),
            P(None, "dp", "tensor"),
            P("tensor", "dp"),
            P("tensor", "dp"),
            P("tensor", "dp"),
            P("tensor", "dp"),
            P("dp", "tensor"),
            P("dp", "tensor"),
            P("dp", "tensor"),
            P("dp", "tensor"),
            P("tensor", "dp"),
            P("tensor", "dp"),
            P("tensor", "dp"),
            P("tensor", "dp"),
            P(None, "dp"),
            P(None, "dp"),
            P(None, "dp"),
            P(None, "dp"),
        ),
        check_vma=False,
    )
```

profile of v0, /device:TPU:0, one launch (start us, length us, event | category | flops | bytes accessed | tf_op | source)
XLA Modules:
  0.0 818.7 jit_solution(9086663741849592017)
XLA Ops:
  9.8 38.8 %all_gather.15 = bf16[3,768,192]{2,0,1:T(4,128)(2,1)S(1)} all-gather(bf16[3,96,192]{2,0,1:T(4,128)(2,1)S(1)} %copy.117), channel_id=1, replica_groups=mesh['dp'=8,'tensor'=4] {'dp'}, dimensions={1}, use_global_device_ids=true | all-gather | bytes 995328 | tf_op jit(solution)/shard_map/all_gather | solution.py:71
  48.6 4.4 fusion.39
  54.1 2.4 fusion.2
  56.5 2.2 exponential_reduce_fusion
  60.6 5.3 fusion.58
  66.7 31.2 %all_gather.16 = bf16[192,768]{0,1:T(8,128)(2,1)S(1)} all-gather(bf16[192,96]{0,1:T(8,128)(2,1)S(1)} %copy.124), channel_id=1, replica_groups=mesh['dp'=8,'tensor'=4] {'dp'}, dimensions={1}, use_global_device_ids=true | all-gather | bytes 331776 | tf_op jit(solution)/shard_map/all_gather | solution.py:72
  97.9 3.0 fusion.127
  102.2 18.7 %all-gather = bf16[8,96,4]{1,2,0:T(4,128)(2,1)S(1)} all-gather(bf16[1,96,4]{1,2,0:T(4,128)(2,1)S(1)} %bitcast.84), channel_id=1, replica_groups=mesh['dp'=8,'tensor'=4] {'dp'}, dimensions={0}, use_global_device_ids=true | all-gather | bytes 6912 | tf_op jit(solution)/shard_map/all_gather | solution.py:75
  121.0 73.1 %all-reduce.5.cloned.1.call-done = f32[1536,768]{1,0:T(8,128)} async-done(((f32[1536,768]{1,0:T(8,128)}), f32[1536,768]{1,0:T(8,128)}) %all-reduce.5.cloned.1.call-update) | async-done | bytes 4718608 | tf_op jit(solution)/shard_map/psum | solution.py:107
  194.2 2.9 fusion.125
  200.4 14.3 %multiply_convert_fusion.1 = (bf16[1536,768]{1,0:T(8,128)(2,1)}, f32[1536,768]{1,0:T(8,128)}, f32[1536,768]{1,0:T(8,128)}) fusion(bf16[1536,768]{1,0:T(8,128)(2,1)S(1)} %fusion.38, bf16[768,768]{1,0:T(8,128)(2,1)} %all-gather.4.cloned.1.call-done), kind=kOutput, calls=%fused_computation.26 | convolution fusion | flops 1888616448 | bytes 15335424 | tf_op jit(solution)/shard_map/dot_general | solution.py:112
  214.7 6.3 fusion.128
  221.2 94.1 %all-reduce.7.cloned.1.call-done = f32[1536,768]{1,0:T(8,128)} async-done(((f32[1536,768]{1,0:T(8,128)}), f32[1536,768]{1,0:T(8,128)}) %all-reduce.7.cloned.1.call-update) | async-done | bytes 4718608 | tf_op jit(solution)/shard_map/psum | solution.py:116
  315.3 4.7 fusion.122
  321.6 2.9 multiply_reduce_fusion.1
  324.6 4.4 subtract_multiply_fusion.1
  329.1 3.3 add_convert_fusion
  333.9 4.3 fusion.129
  339.7 92.9 %all-reduce.9.cloned.1.call-done = f32[1536,768]{1,0:T(8,128)} async-done(((f32[1536,768]{1,0:T(8,128)}), f32[1536,768]{1,0:T(8,128)}) %all-reduce.9.cloned.1.call-update) | async-done | bytes 4718608 | tf_op jit(solution)/shard_map/psum | solution.py:129
  432.5 7.1 multiply_reduce_fusion.2
  439.6 3.3 subtract_multiply_fusion
  443.0 2.2 copy-done.1
  445.2 1.8 convolution_convert_fusion.1
  446.9 2.2 reshape.173
  449.1 7.2 fusion.59
  456.3 5.1 fusion.71
  461.4 1.9 convolution_bitcast_fusion.1
  466.3 18.4 %fusion.52 = bf16[3,512,3,64]{1,3,2,0:T(8,128)(2,1)} fusion(f32[3,3,512,512]{2,3,1,0:T(8,128)} %fusion.71, f32[3,3,512,512]{2,3,1,0:T(8,128)} %copy-done.2, f32[3,3,512]{2,1,0:T(4,128)S(1)} %copy-done.26, pred[3,512]{1,0:T(4,128)(4,1)S(1)} %get-tuple-element.155, bf16[3,512,3,64]{1,0,3,2:T(4,128)(2,1)} %copy-done.6), kind=kOutput, calls=%fused_computation.69 | convolution fusion | flops 328242176 | bytes 20073984 | tf_op jit(solution)/shard_map/shqk,sqhe->skhe/dot_general | solution.py:153
  484.7 18.3 %fusion.55 = bf16[3,512,3,64]{1,3,2,0:T(8,128)(2,1)} fusion(f32[3,3,512,512]{2,3,1,0:T(8,128)} %fusion.71, f32[3,3,512,512]{2,3,1,0:T(8,128)} %copy-done.2, f32[3,3,512]{2,1,0:T(4,128)S(1)} %copy-done.26, pred[3,512]{1,0:T(4,128)(4,1)S(1)} %get-tuple-element.155, bf16[3,512,3,64]{1,0,3,2:T(4,128)(2,1)} %copy-done.5), kind=kOutput, calls=%fused_computation.70 | convolution fusion | flops 328242176 | bytes 20073984 | tf_op jit(solution)/shard_map/shqk,skhe->sqhe/dot_general | solution.py:150
  504.4 2.0 stack.29
  506.3 2.5 copy.133
  508.8 2.5 stack.28
  511.3 2.5 copy.130
  513.8 2.5 stack.27
  520.0 5.6 convolution_bitcast_fusion
  525.7 6.5 fusion.62
  532.3 5.1 fusion.130
  537.5 5.0 fusion.43
  542.5 3.2 copy.149
  545.8 2.8 reshape.182
  553.3 39.2 %reduce-scatter.18.cloned.1.call-done = f32[96,192]{1,0:T(8,128)} async-done(((f32[768,192]{1,0:T(8,128)}), f32[96,192]{1,0:T(8,128)}) %reduce-scatter.18.cloned.1.call-update) | async-done | bytes 73744
  595.2 24.7 %all-reduce.11.cloned.1.call-done = f32[1536,768]{1,0:T(8,128)} async-done(((f32[1536,768]{1,0:T(8,128)}), f32[1536,768]{1,0:T(8,128)}) %all-reduce.11.cloned.1.call-update) | async-done | bytes 4718608 | tf_op jit(solution)/shard_map/psum | solution.py:165
  619.9 6.6 add.161
  626.6 38.0 %reduce-scatter.14.cloned.1.call-done = f32[768,96]{0,1:T(8,128)} async-done(((f32[768,768]{0,1:T(8,128)}), f32[768,96]{0,1:T(8,128)}) %reduce-scatter.14.cloned.1.call-update) | async-done | bytes 294928 | tf_op jit(solution)/shard_map/reduce_scatter | solution.py:170
  664.5 2.1 fusion.114
  666.6 69.9 %reduce-scatter.12.cloned.1.call-done = f32[96,768]{1,0:T(8,128)} async-done(((f32[768,768]{1,0:T(8,128)}), f32[96,768]{1,0:T(8,128)}) %reduce-scatter.12.cloned.1.call-update) | async-done | bytes 294928 | tf_op jit(solution)/shard_map/reduce_scatter | solution.py:169
  736.5 2.1 fusion.116
  738.6 67.8 %reduce-scatter.16.cloned.1.call-done = f32[96,576]{1,0:T(8,128)} async-done(((f32[768,576]{1,0:T(8,128)}), f32[96,576]{1,0:T(8,128)}) %reduce-scatter.16.cloned.1.call-update) | async-done | bytes 221200
  (156 shorter events, 34.7 us)
Async XLA Ops:
  8.0 186.1 %all-reduce.5.cloned.1.call-start = ((), (), s32[]{:S(2)}) async-start(), calls=%async_computation.5 | async-start | bytes 9437184 | tf_op jit(solution)/shard_map/psum | solution.py:107
  48.6 4.4 copy-start.12
  53.6 2.8 copy-start.6
  54.1 2.4 copy-start.5
  56.5 3.6 copy-start.2
  60.1 5.8 copy-start.25
  60.6 5.3 copy-start.7
  60.6 6.0 copy-start.21
  97.9 4.3 copy-start.28
  97.9 96.3 %copy-start.10 = (bf16[1536,768]{1,0:T(8,128)(2,1)S(1)}, bf16[1536,768]{1,0:T(8,128)(2,1)}, u32[]{:S(2)}) copy-start(bf16[1536,768]{1,0:T(8,128)(2,1)} %param.20) | copy-start | bytes 7077892
  101.0 99.4 %all-gather.4.cloned.1.call-start = ((), (), s32[]{:S(2)}) async-start(), calls=%async_computation.6 | async-start | bytes 1327104 | tf_op jit(solution)/shard_map/all_gather | solution.py:73
  101.5 113.1 %all-gather.6.cloned.1.call-start = ((), (), s32[]{:S(2)}) async-start(), calls=%async_computation.7 | async-start | bytes 1327104 | tf_op jit(solution)/shard_map/all_gather | solution.py:74
  102.1 213.2 %all-reduce.7.cloned.1.call-start = ((), (), s32[]{:S(2)}) async-start(), calls=%async_computation.8 | async-start | bytes 9437184 | tf_op jit(solution)/shard_map/psum | solution.py:116
  197.0 2.2 copy-start
  221.0 211.6 %all-reduce.9.cloned.1.call-start = ((), (), s32[]{:S(2)}) async-start(), calls=%async_computation.9 | async-start | bytes 9437184 | tf_op jit(solution)/shard_map/psum | solution.py:129
  319.9 1.7 copy-start.4
  321.6 7.4 slice-start.2
  321.6 7.4 slice-start.4
  324.6 4.5 copy-start.33
  324.6 4.5 slice-start.3
  324.6 4.5 slice-start.5
  329.0 3.4 copy-start.3
  329.1 4.8 copy-start.32
  338.2 213.6 %reduce-scatter.20.cloned.1.call-start = ((), (), s32[]{:S(2)}) async-start(), calls=%async_computation.15 | async-start | bytes 442368
  443.0 2.2 copy-start.1
  445.2 4.0 copy-start.26
  446.9 14.5 %slice-start = ((s8[4718592]{0:T(1024)(128)(4,1)}), s8[524288]{0:T(1024)(128)(4,1)S(1)}, s32[]{:S(2)}) async-start(s8[4718592]{0:T(1024)(128)(4,1)} %bitcast.73), calls=%async_computation.16 | async-start | bytes 1048576
  449.1 7.2 copy-start.8
  449.1 7.2 copy-start.9
  449.1 12.3 %slice-start.1 = ((s8[4718592]{0:T(1024)(128)(4,1)}), s8[4194304]{0:T(1024)(128)(4,1)S(1)}, s32[]{:S(2)}) async-start(s8[4718592]{0:T(1024)(128)(4,1)} %bitcast.73), calls=%async_computation.17 | async-start | bytes 8388608
  461.4 2.6 copy-start.27
  465.8 126.8 %reduce-scatter.18.cloned.1.call-start = ((), (), s32[]{:S(2)}) async-start(), calls=%async_computation.14 | async-start | bytes 884736
  484.7 18.3 %copy-start.16 = (bf16[3,512,3,64]{1,3,2,0:T(8,128)(2,1)S(1)}, bf16[3,512,3,64]{1,3,2,0:T(8,128)(2,1)}, u32[]{:S(2)}) copy-start(bf16[3,512,3,64]{1,3,2,0:T(8,128)(2,1)} %fusion.59) | copy-start | bytes 1769476
  516.3 103.6 %all-reduce.11.cloned.1.call-start = ((), (), s32[]{:S(2)}) async-start(), calls=%async_computation.10 | async-start | bytes 9437184 | tf_op jit(solution)/shard_map/psum | solution.py:165
  525.6 138.9 %reduce-scatter.14.cloned.1.call-start = ((), (), s32[]{:S(2)}) async-start(), calls=%async_computation.12 | async-start | bytes 2654208 | tf_op jit(solution)/shard_map/reduce_scatter | solution.py:170
  532.2 204.3 %reduce-scatter.12.cloned.1.call-start = ((), (), s32[]{:S(2)}) async-start(), calls=%async_computation.11 | async-start | bytes 2654208 | tf_op jit(solution)/shard_map/reduce_scatter | solution.py:169
  537.4 268.9 %reduce-scatter.16.cloned.1.call-start = ((), (), s32[]{:S(2)}) async-start(), calls=%async_computation.13 | async-start | bytes 2211840
  545.7 2.9 copy-start.15
  545.7 7.0 copy-start.29
  545.7 7.0 copy-start.30
  545.7 7.0 copy-start.31
  545.8 47.8 %copy-start.23 = (f32[192,96]{1,0:T(8,128)S(1)}, f32[192,96]{1,0:T(8,128)}, u32[]{:S(2)}) copy-start(f32[192,96]{1,0:T(8,128)} %param.36) | copy-start | bytes 221188
  595.2 69.4 %copy-start.13 = (bf16[768,96]{0,1:T(8,128)(2,1)S(1)}, bf16[768,96]{0,1:T(8,128)(2,1)}, u32[]{:S(2)}) copy-start(bf16[768,96]{0,1:T(8,128)(2,1)} %param.28) | copy-start | bytes 442372
  595.2 69.4 %copy-start.17 = (f32[768,96]{0,1:T(8,128)S(1)}, f32[768,96]{0,1:T(8,128)}, u32[]{:S(2)}) copy-start(f32[768,96]{0,1:T(8,128)} %param.38) | copy-start | bytes 884740
  595.2 69.4 %copy-start.18 = (f32[768,96]{0,1:T(8,128)S(1)}, f32[768,96]{0,1:T(8,128)}, u32[]{:S(2)}) copy-start(f32[768,96]{0,1:T(8,128)} %param.33) | copy-start | bytes 884740
  595.2 141.3 %copy-start.14 = (bf16[96,768]{1,0:T(8,128)(2,1)S(1)}, bf16[96,768]{1,0:T(8,128)(2,1)}, u32[]{:S(2)}) copy-start(bf16[96,768]{1,0:T(8,128)(2,1)} %param.27) | copy-start | bytes 442372
  595.2 141.3 %copy-start.19 = (f32[96,768]{1,0:T(8,128)S(1)}, f32[96,768]{1,0:T(8,128)}, u32[]{:S(2)}) copy-start(f32[96,768]{1,0:T(8,128)} %param.37) | copy-start | bytes 884740
  595.2 141.3 %copy-start.20 = (f32[96,768]{1,0:T(8,128)S(1)}, f32[96,768]{1,0:T(8,128)}, u32[]{:S(2)}) copy-start(f32[96,768]{1,0:T(8,128)} %param.32) | copy-start | bytes 884740
  (3 other events, 4.4 us)
Sparse Core Ops, SparseCore 0:
  101.1 93.0 all-reduce.4
  221.1 94.1 all-reduce.6
  338.3 94.1 all-reduce.8
  525.8 94.1 all-reduce.10
Sparse Core Ops, SparseCore 1:
  103.6 40.4 all-gather.3
  146.2 40.0 all-gather.5
  465.8 61.6 reduce-scatter.19
  530.8 61.6 reduce-scatter.17
  596.4 68.0 reduce-scatter.13
  668.4 68.0 reduce-scatter.11
  740.3 66.0 reduce-scatter.15
where the time goes:
time: 826 us; the launch traced here: 819 us
  waiting for transfers between devices  501 us (61%)
  matrix products  118 us (14%)
  blocking collectives  88.7 us (11%)
  local copies, waits for them, and re-layouts  47.8 us (6%)
  other arithmetic  44.7 us (5%)
  between operations  16.9 us (2%)
    unnamed x14, waiting for transfers between devices  108 us
    psum x1, waiting for transfers between devices, on_device(): ffn_total = lax.psum(ffn_part, 'tensor')  94.1 us
    psum x1, waiting for transfers between devices, on_device(): hidden_grad = grad_two + lax.psum(hidden_part, 'tensor')  92.9 us
    psum x1, waiting for transfers between devices, on_device(): attn_total = lax.psum(attn_part, 'tensor')  73.1 us
    reduce_scatter x1, waiting for transfers between devices, on_device(): lax.psum_scatter(grad_up, 'dp', scatter_dimension=0, tiled=True)  69.9 us
    all_gather x1, blocking collectives, on_device(): lax.all_gather(qkv_weight, 'dp', axis=1, tiled=True)  38.8 us
    reduce_scatter x1, waiting for transfers between devices, on_device(): lax.psum_scatter(grad_down, 'dp', scatter_dimension=1, tiled=True)  38 us
    all_gather x1, blocking collectives, on_device(): lax.all_gather(out_weight, 'dp', axis=1, tiled=True)  31.2 us
  transfers between devices with their start and end apart: 11, of which 8 were waited for; matrix products, arithmetic and copies ran while one was open for 14% of the time, Pallas kernels for 0%

commit v1 on v0

--- a/solution.py
+++ b/solution.py
@@ -104,7 +104,7 @@
     )
     context_low = context.reshape(tok_count, local_width).astype(jnp.bfloat16)
     attn_part = jnp.dot(context_low, out_full, preferred_element_type=jnp.float32)
-    attn_total = lax.psum(attn_part, "tensor")
+    attn_total = jnp.sum(lax.all_gather(attn_part, "tensor"), axis=0)
     hidden_one, normed_one, inverse_one = norm_forward(
         tok_float + attn_total, norm_float[0], norm_float[1]
     )

time: 826 us -> 985 us (1.19)
  waiting for transfers between devices: 501 us -> 666 us
  local copies, waits for them, and re-layouts: 47.8 us -> 35 us
  other arithmetic: 44.7 us -> 56.6 us
    all_gather x0 -> x1, waiting for transfers between devices: none -> 98.8 us  [on_device(): attn_total = jnp.sum(lax.all_gather(attn_part, 'tensor'), axis=0)]
    psum x1 -> x0, waiting for transfers between devices: 73.1 us -> none  [on_device(): attn_total = lax.psum(attn_part, 'tensor')]
    psum x1, waiting for transfers between devices: 24.7 us -> 93.4 us  [on_device(): input_grad = grad_one + lax.psum(input_part, 'tensor')]
    reduce_scatter x1, waiting for transfers between devices: 38 us -> 69.1 us  [on_device(): lax.psum_scatter(grad_down, 'dp', scatter_dimension=1, tiled=True)]
    all_gather x1, waiting for transfers between devices: 0.01 us -> 27.8 us  [on_device(): lax.all_gather(down_weight, 'dp', axis=1, tiled=True)]
    all_gather x1, waiting for transfers between devices: 0.03 us -> 26.6 us  [on_device(): lax.all_gather(up_weight, 'dp', axis=0, tiled=True)]
    unnamed x14, waiting for transfers between devices: 108 us -> 93.7 us
    reduce_sum x0 -> x1, other arithmetic: none -> 10.6 us  [on_device(): attn_total = jnp.sum(lax.all_gather(attn_part, 'tensor'), axis=0)]
  transfers between devices with their start and end apart: 11 -> 11, of which waited for: 8 -> 10; matrix products, arithmetic and copies ran while one was open for 14% -> 14% of each run, Pallas kernels for 0% -> 0%
where the time goes in v1:
time: 985 us; the launch traced here: 978 us
  waiting for transfers between devices  666 us (68%)
  matrix products  115 us (12%)
  blocking collectives  88.7 us (9%)
  other arithmetic  56.6 us (6%)
  local copies, waits for them, and re-layouts  35 us (4%)
  between operations  15.5 us (2%)
    all_gather x1, waiting for transfers between devices, on_device(): attn_total = jnp.sum(lax.all_gather(attn_part, 'tensor'), axis=0)  98.8 us
    psum x1, waiting for transfers between devices, on_device(): hidden_grad = grad_two + lax.psum(hidden_part, 'tensor')  94.3 us
    unnamed x14, waiting for transfers between devices  93.7 us
    psum x1, waiting for transfers between devices, on_device(): input_grad = grad_one + lax.psum(input_part, 'tensor')  93.4 us
    psum x1, waiting for transfers between devices, on_device(): ffn_total = lax.psum(ffn_part, 'tensor')  92.7 us
    reduce_scatter x1, waiting for transfers between devices, on_device(): lax.psum_scatter(grad_up, 'dp', scatter_dimension=0, tiled=True)  69.9 us
    reduce_scatter x1, waiting for transfers between devices, on_device(): lax.psum_scatter(grad_down, 'dp', scatter_dimension=1, tiled=True)  69.1 us
    all_gather x1, blocking collectives, on_device(): lax.all_gather(qkv_weight, 'dp', axis=1, tiled=True)  38.8 us
  transfers between devices with their start and end apart: 11, of which 10 were waited for; matrix products, arithmetic and copies ran while one was open for 14% of the time, Pallas kernels for 0%

profile of v1, /device:TPU:0, one launch (start us, length us, event | category | flops | bytes accessed | tf_op | source)
XLA Modules:
  0.0 978.1 jit_solution(5528566863963331126)
XLA Ops:
  9.0 38.8 %all_gather.21 = bf16[3,768,192]{2,0,1:T(4,128)(2,1)S(1)} all-gather(bf16[3,96,192]{2,0,1:T(4,128)(2,1)S(1)} %copy.117), channel_id=1, replica_groups=mesh['dp'=8,'tensor'=4] {'dp'}, dimensions={1}, use_global_device_ids=true | all-gather | bytes 995328 | tf_op jit(solution)/shard_map/all_gather | solution.py:71
  47.8 4.4 fusion.39
  53.2 2.4 fusion.2
  55.7 2.2 exponential_reduce_fusion
  57.9 1.5 copy-done.2
  59.9 5.3 fusion.58
  66.0 31.2 %all_gather.22 = bf16[192,768]{0,1:T(8,128)(2,1)S(1)} all-gather(bf16[192,96]{0,1:T(8,128)(2,1)S(1)} %copy.124), channel_id=1, replica_groups=mesh['dp'=8,'tensor'=4] {'dp'}, dimensions={1}, use_global_device_ids=true | all-gather | bytes 331776 | tf_op jit(solution)/shard_map/all_gather | solution.py:72
  97.2 3.0 fusion.127
  101.8 18.7 %all-gather.1 = bf16[8,96,4]{1,2,0:T(4,128)(2,1)S(1)} all-gather(bf16[1,96,4]{1,2,0:T(4,128)(2,1)S(1)} %bitcast.84), channel_id=1, replica_groups=mesh['dp'=8,'tensor'=4] {'dp'}, dimensions={0}, use_global_device_ids=true | all-gather | bytes 6912 | tf_op jit(solution)/shard_map/all_gather | solution.py:75
  120.6 98.8 %all-gather.10.cloned.1.call-done = f32[6144,768]{1,0:T(8,128)} async-done(((f32[1536,768]{1,0:T(8,128)}), f32[6144,768]{1,0:T(8,128)}) %all-gather.10.cloned.1.call-update) | async-done | bytes 18874384 | tf_op jit(solution)/shard_map/all_gather | solution.py:107
  219.4 10.6 %reduce_sum.136 = f32[1536,768]{1,0:T(8,128)} reduce(f32[4,1536,768]{2,1,0:T(8,128)} %bitcast.74, f32[]{:T(128)} %constant.52.clone.1), dimensions={0}, to_apply=%region_2.3 | reduce | flops 3538944 | bytes 23592964 | tf_op jit(solution)/shard_map/reduce_sum | solution.py:107
  229.9 2.9 fusion.125
  236.0 26.6 %all-gather.6.cloned.1.call-done = bf16[768,768]{1,0:T(8,128)(2,1)} async-done(((bf16[96,768]{1,0:T(8,128)(2,1)}), bf16[768,768]{1,0:T(8,128)(2,1)}) %all-gather.6.cloned.1.call-update) | async-done | bytes 1179664 | tf_op jit(solution)/shard_map/all_gather | solution.py:73
  262.6 14.3 %multiply_convert_fusion.1 = (bf16[1536,768]{1,0:T(8,128)(2,1)}, f32[1536,768]{1,0:T(8,128)}, f32[1536,768]{1,0:T(8,128)}) fusion(bf16[1536,768]{1,0:T(8,128)(2,1)S(1)} %fusion.38, bf16[768,768]{1,0:T(8,128)(2,1)} %all-gather.6.cloned.1.call-done), kind=kOutput, calls=%fused_computation.26 | convolution fusion | flops 1888616448 | bytes 15335424 | tf_op jit(solution)/shard_map/dot_general | solution.py:112
  276.9 27.8 %all-gather.8.cloned.1.call-done = bf16[768,768]{0,1:T(8,128)(2,1)} async-done(((bf16[768,96]{0,1:T(8,128)(2,1)}), bf16[768,768]{0,1:T(8,128)(2,1)}) %all-gather.8.cloned.1.call-update) | async-done | bytes 1179664 | tf_op jit(solution)/shard_map/all_gather | solution.py:74
  304.7 6.1 fusion.128
  311.1 92.7 %all-reduce.4.cloned.1.call-done = f32[1536,768]{1,0:T(8,128)} async-done(((f32[1536,768]{1,0:T(8,128)}), f32[1536,768]{1,0:T(8,128)}) %all-reduce.4.cloned.1.call-update) | async-done | bytes 4718608 | tf_op jit(solution)/shard_map/psum | solution.py:116
  403.8 4.7 fusion.122
  410.1 2.9 multiply_reduce_fusion.1
  413.1 4.4 subtract_multiply_fusion.1
  417.6 3.3 add_convert_fusion
  422.3 4.3 fusion.129
  426.7 94.3 %all-reduce.6.cloned.1.call-done = f32[1536,768]{1,0:T(8,128)} async-done(((f32[1536,768]{1,0:T(8,128)}), f32[1536,768]{1,0:T(8,128)}) %all-reduce.6.cloned.1.call-update) | async-done | bytes 4718608 | tf_op jit(solution)/shard_map/psum | solution.py:129
  521.0 7.7 multiply_reduce_fusion.2
  529.7 4.6 subtract_multiply_fusion
  534.4 2.2 copy-done.1
  536.5 2.0 convolution_bitcast_fusion.1
  538.6 6.5 fusion.62
  545.2 5.2 fusion.130
  550.9 3.3 convolution_convert_fusion.1
  554.6 6.1 fusion.59
  562.1 5.1 fusion.71
  567.1 16.9 %fusion.52 = bf16[3,512,3,64]{1,3,2,0:T(8,128)(2,1)S(1)} fusion(f32[3,3,512,512]{2,3,1,0:T(8,128)} %fusion.71, f32[3,3,512,512]{2,3,1,0:T(8,128)} %copy-done.2, f32[3,3,512]{2,1,0:T(4,128)S(1)} %log_add_fusion, pred[3,512]{1,0:T(4,128)(4,1)S(1)} %get-tuple-element.155, bf16[3,512,3,64]{1,0,3,2:T(4,128)(2,1)S(1)} %copy-done.8), kind=kOutput, calls=%fused_computation.69 | convolution fusion | flops 328242176 | bytes 20073984 | tf_op jit(solution)/shard_map/shqk,sqhe->skhe/dot_general | solution.py:153
  585.5 16.9 %fusion.55 = bf16[3,512,3,64]{1,3,2,0:T(8,128)(2,1)S(1)} fusion(f32[3,3,512,512]{2,3,1,0:T(8,128)} %fusion.71, f32[3,3,512,512]{2,3,1,0:T(8,128)} %copy-done.2, f32[3,3,512]{2,1,0:T(4,128)} %copy-done.23, pred[3,512]{1,0:T(4,128)(4,1)S(1)} %get-tuple-element.155, bf16[3,512,3,64]{1,0,3,2:T(4,128)(2,1)S(1)} %copy-done.6), kind=kOutput, calls=%fused_computation.70 | convolution fusion | flops 328242176 | bytes 20073984 | tf_op jit(solution)/shard_map/shqk,skhe->sqhe/dot_general | solution.py:150
  605.2 5.6 convolution_bitcast_fusion
  610.9 1.6 copy-done.12
  612.5 4.2 fusion.43
  616.8 3.0 copy.149
  619.8 2.8 reshape.183
  628.3 28.0 %reduce-scatter.18.cloned.1.call-done = f32[96,192]{1,0:T(8,128)} async-done(((f32[768,192]{1,0:T(8,128)}), f32[96,192]{1,0:T(8,128)}) %reduce-scatter.18.cloned.1.call-update) | async-done | bytes 73744
  657.3 1.7 fusion.118
  659.0 69.1 %reduce-scatter.14.cloned.1.call-done = f32[768,96]{0,1:T(8,128)} async-done(((f32[768,768]{0,1:T(8,128)}), f32[768,96]{0,1:T(8,128)}) %reduce-scatter.14.cloned.1.call-update) | async-done | bytes 294928 | tf_op jit(solution)/shard_map/reduce_scatter | solution.py:170
  728.1 2.2 fusion.114
  730.3 69.9 %reduce-scatter.12.cloned.1.call-done = f32[96,768]{1,0:T(8,128)} async-done(((f32[768,768]{1,0:T(8,128)}), f32[96,768]{1,0:T(8,128)}) %reduce-scatter.12.cloned.1.call-update) | async-done | bytes 294928 | tf_op jit(solution)/shard_map/reduce_scatter | solution.py:169
  800.2 2.1 fusion.116
  802.3 93.4 %all-reduce.8.cloned.1.call-done = f32[1536,768]{1,0:T(8,128)} async-done(((f32[1536,768]{1,0:T(8,128)}), f32[1536,768]{1,0:T(8,128)}) %all-reduce.8.cloned.1.call-update) | async-done | bytes 4718608 | tf_op jit(solution)/shard_map/psum | solution.py:165
  895.7 6.6 add.159
  902.3 64.2 %reduce-scatter.16.cloned.1.call-done = f32[96,576]{1,0:T(8,128)} async-done(((f32[768,576]{1,0:T(8,128)}), f32[96,576]{1,0:T(8,128)}) %reduce-scatter.16.cloned.1.call-update) | async-done | bytes 221200
  (142 shorter events, 30.8 us)
Async XLA Ops:
  7.2 212.2 %all-gather.10.cloned.1.call-start = ((), (), s32[]{:S(2)}) async-start(), calls=%async_computation.12 | async-start | bytes 23592960 | tf_op jit(solution)/shard_map/all_gather | solution.py:107
  47.8 4.4 copy-start.14
  52.8 2.8 copy-start.7
  53.2 2.4 copy-start.5
  55.6 3.7 copy-start.2
  59.4 507.8 %copy-start.23 = (f32[3,3,512]{2,1,0:T(4,128)}, f32[3,3,512]{2,1,0:T(4,128)S(1)}, u32[]{:S(2)}) copy-start(f32[3,3,512]{2,1,0:T(4,128)S(1)} %log_add_fusion) | copy-start | bytes 55300
  59.8 5.3 copy-start.9
  59.8 6.0 copy-start.19
  97.2 4.6 copy-start.24
  100.2 162.4 %all-gather.6.cloned.1.call-start = ((), (), s32[]{:S(2)}) async-start(), calls=%async_computation.5 | async-start | bytes 1327104 | tf_op jit(solution)/shard_map/all_gather | solution.py:73
  101.0 203.7 %all-gather.8.cloned.1.call-start = ((), (), s32[]{:S(2)}) async-start(), calls=%async_computation.6 | async-start | bytes 1327104 | tf_op jit(solution)/shard_map/all_gather | solution.py:74
  101.7 302.1 %all-reduce.4.cloned.1.call-start = ((), (), s32[]{:S(2)}) async-start(), calls=%async_computation.7 | async-start | bytes 9437184 | tf_op jit(solution)/shard_map/psum | solution.py:116
  219.4 10.6 %copy-start.11 = (bf16[1536,768]{1,0:T(8,128)(2,1)S(1)}, bf16[1536,768]{1,0:T(8,128)(2,1)}, u32[]{:S(2)}) copy-start(bf16[1536,768]{1,0:T(8,128)(2,1)} %param.20) | copy-start | bytes 7077892
  232.8 2.1 copy-start
  310.9 210.1 %all-reduce.6.cloned.1.call-start = ((), (), s32[]{:S(2)}) async-start(), calls=%async_computation.8 | async-start | bytes 9437184 | tf_op jit(solution)/shard_map/psum | solution.py:129
  408.5 1.7 copy-start.4
  408.5 1.7 copy-start.22
  410.1 7.4 slice-start
  410.1 7.4 slice-start.2
  413.1 4.5 copy-start.28
  413.1 4.5 slice-start.1
  413.1 4.5 slice-start.3
  417.5 3.4 copy-start.3
  417.6 4.7 copy-start.27
  420.9 1.4 copy-start.13
  426.6 200.1 %reduce-scatter.20.cloned.1.call-start = ((), (), s32[]{:S(2)}) async-start(), calls=%async_computation.15 | async-start | bytes 442368
  529.7 126.6 %reduce-scatter.18.cloned.1.call-start = ((), (), s32[]{:S(2)}) async-start(), calls=%async_computation.14 | async-start | bytes 884736
  534.3 2.2 copy-start.1
  538.5 189.6 %reduce-scatter.14.cloned.1.call-start = ((), (), s32[]{:S(2)}) async-start(), calls=%async_computation.11 | async-start | bytes 2654208 | tf_op jit(solution)/shard_map/reduce_scatter | solution.py:170
  545.1 255.1 %reduce-scatter.12.cloned.1.call-start = ((), (), s32[]{:S(2)}) async-start(), calls=%async_computation.10 | async-start | bytes 2654208 | tf_op jit(solution)/shard_map/reduce_scatter | solution.py:169
  550.4 345.3 %all-reduce.8.cloned.1.call-start = ((), (), s32[]{:S(2)}) async-start(), calls=%async_computation.9 | async-start | bytes 9437184 | tf_op jit(solution)/shard_map/psum | solution.py:165
  554.6 7.4 copy-start.10
  562.1 5.1 copy-start.8
  567.1 18.3 %copy-start.6 = (bf16[3,512,3,64]{1,0,3,2:T(4,128)(2,1)S(1)}, bf16[3,512,3,64]{1,0,3,2:T(4,128)(2,1)}, u32[]{:S(2)}) copy-start(bf16[3,512,3,64]{1,0,3,2:T(4,128)(2,1)} %copy-done.5) | copy-start | bytes 1769476
  604.0 1.2 copy-start.21
  610.9 1.7 copy-start.12
  610.9 355.6 %reduce-scatter.16.cloned.1.call-start = ((), (), s32[]{:S(2)}) async-start(), calls=%async_computation.13 | async-start | bytes 2211840
  619.7 7.9 copy-start.25
  619.7 7.9 copy-start.26
  619.8 37.5 %copy-start.20 = (bf16[192,96]{1,0:T(8,128)(2,1)S(1)}, bf16[192,96]{1,0:T(8,128)(2,1)}, u32[]{:S(2)}) copy-start(bf16[192,96]{1,0:T(8,128)(2,1)} %param.26) | copy-start | bytes 110596
  619.8 108.3 %copy-start.15 = (bf16[768,96]{0,1:T(8,128)(2,1)S(1)}, bf16[768,96]{0,1:T(8,128)(2,1)}, u32[]{:S(2)}) copy-start(bf16[768,96]{0,1:T(8,128)(2,1)} %param.28) | copy-start | bytes 442372
  619.8 180.5 %copy-start.16 = (bf16[96,768]{1,0:T(8,128)(2,1)S(1)}, bf16[96,768]{1,0:T(8,128)(2,1)}, u32[]{:S(2)}) copy-start(bf16[96,768]{1,0:T(8,128)(2,1)} %param.27) | copy-start | bytes 442372
  622.6 177.6 %copy-start.17 = (f32[96,768]{1,0:T(8,128)S(1)}, f32[96,768]{1,0:T(8,128)}, u32[]{:S(2)}) copy-start(f32[96,768]{1,0:T(8,128)} %param.37) | copy-start | bytes 884740
  622.6 177.6 %copy-start.18 = (f32[96,768]{1,0:T(8,128)S(1)}, f32[96,768]{1,0:T(8,128)}, u32[]{:S(2)}) copy-start(f32[96,768]{1,0:T(8,128)} %param.32) | copy-start | bytes 884740
Sparse Core Ops, SparseCore 0:
  100.3 118.9 all-gather.9
  221.6 41.0 all-gather.5
  264.8 39.8 all-gather.7
  311.0 92.7 all-reduce.3
  426.8 94.1 all-reduce.5
  529.8 61.5 reduce-scatter.19
  594.6 61.6 reduce-scatter.17
  660.2 67.8 reduce-scatter.13
  732.0 68.1 reduce-scatter.11
  802.6 93.0 all-reduce.7
  899.6 66.7 reduce-scatter.15
